TPU v7x, 512 devices: a whole 4x4x16 slice. The times are simulated.
512 devices in a mesh: dp: 64 (over z, y_hi, core), blk: 8 (over y_lo, x).
Axes of the slice: x: 4, y: 4 (y_hi: 2, y_lo: 2; y = y_hi * 2 + y_lo), z: 16, core: 2. Of those that a mesh axis runs over, the one named last changes fastest.
Arguments:
- inputs: bfloat16 [20480, 16384], P('dp', 'blk'), may hold values from -6 to 6
- left_factor: bfloat16 [128, 128, 128], P('blk'), may hold values from -0.5 to 0.5
- right_factor: bfloat16 [128, 128, 128], P('blk'), may hold values from -0.5 to 0.5
- grad_output: bfloat16 [20480, 16384], P('dp', 'blk'), may hold values from -6 to 6
Outputs:
- grad_in: bfloat16 [20480, 16384], P('dp', 'blk')
- grad_left: float32 [128, 128, 128], P('blk', 'dp')
- grad_right: float32 [128, 128, 128], P('blk', 'dp')
All inputs are finite; a program needn't handle non-finite values.
Results may differ from a plain program's by a relative error of at most 0.0049.
Values may be sent and summed in bfloat16 or wider, within the bound.
A program may use at most 64 MiB of HBM per device.

v0:
```python
import jax
import jax.numpy as jnp
from jax import lax
from jax.sharding import PartitionSpec as P


def local(inputs, left_factor, right_factor, grad_output):
    groups = lax.axis_size("blk")
    replicas = lax.axis_size("dp")
    tokens_here = inputs.shape[0]
    owned = left_factor.shape[0]
    width_block = left_factor.shape[1]
    loss_scale = float(tokens_here * replicas) ** (-0.5)
    features = inputs.reshape(tokens_here, owned, width_block)
    upstream = grad_output.reshape(tokens_here, owned, width_block)
    left_view = left_factor.reshape(owned, width_block, groups, owned)
    right_view = right_factor.reshape(owned, groups, owned, width_block)
    hidden = jnp.einsum("tci,cibj->btcj", features, left_view, preferred_element_type=jnp.float32)
    hidden_send = hidden.astype(jnp.bfloat16).reshape(groups, tokens_here, owned * owned)
    back = jnp.einsum("tjm,jbcm->btcj", upstream, right_view, preferred_element_type=jnp.float32)
    back_send = back.astype(jnp.bfloat16).reshape(groups, tokens_here, owned * owned)
    hidden_recv = lax.all_to_all(hidden_send, "blk", split_axis=0, concat_axis=0, tiled=True)
    hidden_four = hidden_recv.reshape(groups, tokens_here, owned, owned)
    right_term = jnp.einsum(
        "btcj,tjm->jbcm", hidden_four, upstream, preferred_element_type=jnp.float32
    )
    right_term = right_term.reshape(owned, groups * owned, width_block) * loss_scale
    piece = lax.all_to_all(back_send, "blk", split_axis=0, concat_axis=0, tiled=True)
    count = piece.shape[1]
    piece_four = piece.reshape(groups, count, owned, owned)
    grad_piece = jnp.einsum(
        "btcj,cibj->tci", piece_four, left_view, preferred_element_type=jnp.float32
    )
    grad_piece = grad_piece.astype(jnp.bfloat16).reshape(count, owned * width_block)
    token_major = jnp.transpose(piece_four, (1, 0, 2, 3))
    left_term = jnp.einsum(
        "tci,tbcj->cibj", features, token_major, preferred_element_type=jnp.float32
    )
    left_term = left_term.reshape(owned, width_block, groups * owned) * loss_scale
    left_summed, right_summed = (
        lax.psum_scatter(left_term, "dp", scatter_dimension=1, tiled=True),
        lax.psum_scatter(right_term, "dp", scatter_dimension=1, tiled=True),
    )
    return (grad_piece, left_summed, right_summed)


def solution(mesh):
    return jax.shard_map(
        local,
        mesh=mesh,
        in_specs=(P("dp", "blk"), P("blk", None, None), P("blk", None, None), P("dp", "blk")),
        out_specs=(P("dp", "blk"), P("blk", "dp", None), P("blk", "dp", None)),
        check_vma=False,
    )
```

profile of v0, /device:TPU:2, one launch (start us, length us, event | category | flops | bytes accessed | tf_op | source)
XLA Modules:
  0.0 479.4 jit_solution(5028669658705305729)
XLA Ops:
  7.2 0.0 copy-start
  7.2 0.0 copy-start.4
  7.2 1.7 copy.59
  8.9 0.0 copy-done.4
  8.9 0.3 copy.30
  9.2 0.8 copy-done.1
  10.0 0.7 fusion.6
  10.7 0.2 copy.37
  10.8 1.6 copy.38
  12.4 10.0 %all-to-all-start.1 = ((bf16[8,320,256]{2,1,0:T(8,128)(2,1)}), bf16[8,320,256]{2,1,0:T(8,128)(2,1)}, u32[]{:S(2)}, u32[]{:S(2)}) async-start(bf16[8,320,256]{2,1,0:T(8,128)(2,1)} %copy.38), calls=%async_computation.2 | async-start | bytes 2621440 | tf_op jit(solution)/shard_map/all_to_all | solution.py:22
  22.4 0.0 reduce-scatter.5.cloned.1.call-start
  22.4 1.6 copy.58
  24.1 11.7 %all-to-all-done.1 = bf16[8,320,256]{2,1,0:T(8,128)(2,1)} async-done(((bf16[8,320,256]{2,1,0:T(8,128)(2,1)}), bf16[8,320,256]{2,1,0:T(8,128)(2,1)}, u32[]{:S(2)}, u32[]{:S(2)}) %all-to-all-start.1) | async-done | bytes 1310752 | tf_op jit(solution)/shard_map/all_to_all | solution.py:22
  35.8 2.6 copy.39
  38.3 2.5 fusion.8
  40.8 1.6 copy.42
  42.4 0.0 reduce-scatter.5.cloned.1.call-update
  42.4 0.0 reduce-scatter.3.cloned.1.call-start
  42.4 0.7 fusion.5
  43.1 0.9 copy.27
  44.1 1.6 copy.28
  45.6 20.5 %all_to_all.10 = bf16[8,320,256]{2,1,0:T(8,128)(2,1)S(1)} all-to-all(bf16[8,320,256]{2,1,0:T(8,128)(2,1)} %copy.28), channel_id=1, replica_groups=mesh['dp'=64,'blk'=8] {'blk'}, dimensions={0} | all-to-all | bytes 2621440 | tf_op jit(solution)/shard_map/all_to_all | solution.py:28
  66.2 1.6 copy.29
  67.7 3.1 fusion.11
  70.8 2.8 copy.35
  73.6 0.0 reduce-scatter.3.cloned.1.call-update
  73.6 0.6 fusion.7
  74.3 1.4 copy.81
  75.7 181.6 %reduce-scatter.5.cloned.1.call-done = f32[16,2,128]{2,0,1:T(8,128)} async-done(((f32[16,128,128]{2,0,1:T(8,128)}), f32[16,2,128]{2,0,1:T(8,128)}) %reduce-scatter.5.cloned.1.call-update) | async-done | bytes 16400 | tf_op jit(solution)/shard_map/reduce_scatter | solution.py:42
  257.3 1.3 copy.44
  258.6 212.6 %reduce-scatter.3.cloned.1.call-done = f32[16,2,128]{2,0,1:T(8,128)} async-done(((f32[16,128,128]{2,0,1:T(8,128)}), f32[16,2,128]{2,0,1:T(8,128)}) %reduce-scatter.3.cloned.1.call-update) | async-done | bytes 16400 | tf_op jit(solution)/shard_map/reduce_scatter | solution.py:41
  471.2 1.3 copy.43
  (6 shorter events, 0.0 us)
Async XLA Ops:
  7.2 35.3 %copy-start = (bf16[16,128,128]{2,1,0:T(8,128)(2,1)S(1)}, bf16[16,128,128]{2,1,0:T(8,128)(2,1)}, u32[]{:S(2)}) copy-start(bf16[16,128,128]{2,1,0:T(8,128)(2,1)} %param.6) | copy-start | bytes 1572868
  7.2 1.7 copy-start.4
  9.2 0.8 copy-start.1
  12.4 23.3 %all-to-all-start.1 = ((bf16[8,320,256]{2,1,0:T(8,128)(2,1)}), bf16[8,320,256]{2,1,0:T(8,128)(2,1)}, u32[]{:S(2)}, u32[]{:S(2)}) async-start(bf16[8,320,256]{2,1,0:T(8,128)(2,1)} %copy.38), calls=%async_computation.2 | async-start | bytes 2621440 | tf_op jit(solution)/shard_map/all_to_all | solution.py:22
  22.4 234.8 %reduce-scatter.5.cloned.1.call-start = ((), (), s32[]{:S(2)}) async-start(), calls=%async_computation.5 | async-start | bytes 1064960 | tf_op jit(solution)/shard_map/reduce_scatter | solution.py:42
  42.4 428.8 %reduce-scatter.3.cloned.1.call-start = ((), (), s32[]{:S(2)}) async-start(), calls=%async_computation.4 | async-start | bytes 1064960 | tf_op jit(solution)/shard_map/reduce_scatter | solution.py:41
  70.8 2.8 copy-start.2
  70.8 2.8 copy-start.3
Sparse Core Ops, SparseCore 0:
  42.5 214.7 reduce-scatter.4
  261.9 209.2 reduce-scatter.2
where the time goes:
time: 480 us; the launch traced here: 479 us
  waiting for transfers between devices  406 us (85%)
  local copies, waits for them, and re-layouts  21.2 us (4%)
  blocking collectives  20.5 us (4%)
  between operations  14.2 us (3%)
  starting transfers between devices  10.1 us (2%)
  matrix products  7.53 us (2%)
    reduce_scatter x1, waiting for transfers between devices, local(): lax.psum_scatter(left_term, 'dp', scatter_dimension=1, tiled=True)  213 us
    reduce_scatter x1, waiting for transfers between devices, local(): lax.psum_scatter(right_term, 'dp', scatter_dimension=1, tiled=True)  182 us
    all_to_all x1, blocking collectives, local(): lax.all_to_all(back_send, 'blk', split_axis=0, concat_axis=0, tiled=True)  20.5 us
    all_to_all x1, waiting for transfers between devices, local(): lax.all_to_all(hidden_send, 'blk', split_axis=0, concat_axis=0, tiled=True)  11.7 us
    all_to_all x1, starting transfers between devices, local(): lax.all_to_all(hidden_send, 'blk', split_axis=0, concat_axis=0, tiled=True)  10 us
  transfers between devices with their start and end apart: 3, of which 3 were waited for; matrix products, arithmetic and copies ran while one was open for 3% of the time, Pallas kernels for 0%

commit v1 on v0

--- a/solution.py
+++ b/solution.py
@@ -1,7 +1,144 @@
+import functools
+
 import jax
 import jax.numpy as jnp
 from jax import lax
+from jax.experimental import pallas as pl
+from jax.experimental.pallas import tpu as pltpu
 from jax.sharding import PartitionSpec as P
+
+MESH = pl.DeviceIdType.MESH
+
+
+def reduce_kernel(
+    scale, rings, l_ref, r_ref, lo_ref, ro_ref, pair, up, down, fold,
+    pair_s, pair_r, up_s, up_r, down_s, down_r, fold_s, fold_r,
+):
+    me = lax.axis_index("dp")
+    core, high, z = lax.rem(me, 2), lax.rem(me // 2, 2), me // 4
+    half = rings // 2
+    mate = me + 1 - 2 * core
+    across = me + 2 - 4 * high
+    above = lax.rem(z + 1, rings) * 4 + high * 2 + core
+    below = lax.rem(z + rings - 1, rings) * 4 + high * 2 + core
+    lanes = (r_ref, l_ref)
+    outs = (ro_ref, lo_ref)
+
+    barrier = pltpu.get_barrier_semaphore()
+    for peer in (mate, across, above, below):
+        pl.semaphore_signal(barrier, inc=1, device_id={"dp": peer}, device_id_type=MESH)
+    pl.semaphore_wait(barrier, 4)
+
+    order = []
+    for step in range(half):
+        order.append(lax.rem(z + half - step, rings))
+        if step < half - 1:
+            order.append(lax.rem(z + rings - (half - 1 - step), rings))
+    order.append(z)
+
+    def send(src, dst, send_sem, recv_sem, peer):
+        copy = pltpu.make_async_remote_copy(
+            src_ref=src, dst_ref=dst, send_sem=send_sem, recv_sem=recv_sem,
+            device_id={"dp": peer}, device_id_type=MESH,
+        )
+        copy.start()
+        return copy
+
+    pairs = [[None] * rings for _ in lanes]
+    for k, target in enumerate(order):
+        for lane, ref in enumerate(lanes):
+            pairs[lane][k] = send(
+                ref.at[target, :, 1 - core], pair.at[lane, k],
+                pair_s.at[lane, k], pair_r.at[lane, k], mate,
+            )
+
+    started = []
+
+    def own(lane, k):
+        pairs[lane][k].wait_recv()
+        return pair[lane, k] + lanes[lane][order[k], :, core]
+
+    ups, downs = [None, None], [None, None]
+    for step in range(half):
+        for lane in range(2):
+            k = 2 * step
+            mine = own(lane, k)
+            if step == 0:
+                source = pair.at[lane, k]
+                source[...] = mine
+            else:
+                ups[lane].wait_recv()
+                source = up.at[lane, step - 1]
+                source[...] += mine
+            ups[lane] = send(source, up.at[lane, step], up_s.at[lane, step], up_r.at[lane, step], above)
+            started.append(ups[lane])
+            if step < half - 1:
+                k = 2 * step + 1
+                mine = own(lane, k)
+                if step == 0:
+                    source = pair.at[lane, k]
+                    source[...] = mine
+                else:
+                    downs[lane].wait_recv()
+                    source = down.at[lane, step - 1]
+                    source[...] += mine
+                downs[lane] = send(
+                    source, down.at[lane, step], down_s.at[lane, step], down_r.at[lane, step], below
+                )
+                started.append(downs[lane])
+
+    folds = []
+    for lane in range(2):
+        mine = own(lane, rings - 1)
+        ups[lane].wait_recv()
+        downs[lane].wait_recv()
+        pair[lane, rings - 1] = mine + up[lane, half - 1] + down[lane, half - 2]
+        folds.append(
+            send(pair.at[lane, rings - 1, 1 - high], fold.at[lane], fold_s.at[lane], fold_r.at[lane], across)
+        )
+    for lane in range(2):
+        folds[lane].wait_recv()
+        outs[lane][...] = (pair[lane, rings - 1, high] + fold[lane]) * scale
+    for copies in (*pairs, started, folds):
+        for copy in copies:
+            copy.wait_send()
+
+
+def reduce_both(left_term, right_term, scale, replicas):
+    owned, width, _ = left_term.shape
+    rings = replicas // 4
+    half = rings // 2
+    rows = owned * (width // replicas)
+
+    def arrange(term):
+        return jnp.transpose(term, (1, 0, 2)).reshape(rings, 2, 2, rows, width)
+
+    dma = pltpu.SemaphoreType.DMA
+    vmem = pl.BlockSpec(memory_space=pltpu.VMEM)
+    piece = (2, rows, width)
+    left, right = pl.pallas_call(
+        functools.partial(reduce_kernel, scale, rings),
+        out_shape=[jax.ShapeDtypeStruct((rows, width), jnp.float32)] * 2,
+        in_specs=[vmem, vmem],
+        out_specs=[vmem, vmem],
+        scratch_shapes=[
+            pltpu.VMEM((2, rings) + piece, jnp.float32),
+            pltpu.VMEM((2, half) + piece, jnp.float32),
+            pltpu.VMEM((2, half - 1) + piece, jnp.float32),
+            pltpu.VMEM((2, rows, width), jnp.float32),
+            dma((2, rings)), dma((2, rings)),
+            dma((2, half)), dma((2, half)),
+            dma((2, half - 1)), dma((2, half - 1)),
+            dma((2,)), dma((2,)),
+        ],
+        compiler_params=pltpu.CompilerParams(collective_id=0, has_side_effects=True),
+        name="reduce_over_dp",
+    )(arrange(left_term), arrange(right_term))
+
+    def restore(out):
+        return jnp.transpose(out.reshape(width // replicas, owned, width), (1, 0, 2))
+
+    return restore(left), restore(right)
 
 
 def local(inputs, left_factor, right_factor, grad_output):
@@ -24,7 +161,7 @@
     right_term = jnp.einsum(
         "btcj,tjm->jbcm", hidden_four, upstream, preferred_element_type=jnp.float32
     )
-    right_term = right_term.reshape(owned, groups * owned, width_block) * loss_scale
+    right_term = right_term.reshape(owned, groups * owned, width_block)
     piece = lax.all_to_all(back_send, "blk", split_axis=0, concat_axis=0, tiled=True)
     count = piece.shape[1]
     piece_four = piece.reshape(groups, count, owned, owned)
@@ -36,11 +173,8 @@
     left_term = jnp.einsum(
         "tci,tbcj->cibj", features, token_major, preferred_element_type=jnp.float32
     )
-    left_term = left_term.reshape(owned, width_block, groups * owned) * loss_scale
-    left_summed, right_summed = (
-        lax.psum_scatter(left_term, "dp", scatter_dimension=1, tiled=True),
-        lax.psum_scatter(right_term, "dp", scatter_dimension=1, tiled=True),
-    )
+    left_term = left_term.reshape(owned, width_block, groups * owned)
+    left_summed, right_summed = reduce_both(left_term, right_term, loss_scale, replicas)
     return (grad_piece, left_summed, right_summed)
 
 

time: 480 us -> 106 us (0.22)
  waiting for transfers between devices: 406 us -> 13.8 us
  Pallas kernels: 0 us -> 47 us
  blocking collectives: 20.5 us -> 0 us
  between operations: 14.2 us -> 0.74 us
  starting transfers between devices: 10.1 us -> 15.3 us
    reduce_scatter x2 -> x0, waiting for transfers between devices: 394 us -> none  [the longest x1 213 us: local(): lax.psum_scatter(left_term, 'dp', scatter_dimension=1, tiled=True)]
    pallas_call x0 -> x1, Pallas kernels: none -> 47 us  [reduce_both(): pl.pallas_call(functools.partial(reduce_kernel, scale, rings), out_shape=...]
    all_to_all x1 -> x0, blocking collectives: 20.5 us -> none  [local(): lax.all_to_all(back_send, 'blk', split_axis=0, concat_axis=0, tiled=True)]
    all_to_all x0 -> x1, starting transfers between devices: none -> 10 us  [local(): lax.all_to_all(back_send, 'blk', split_axis=0, concat_axis=0, tiled=True)]
    all_to_all x0 -> x1, waiting for transfers between devices: none -> 5.78 us  [local(): lax.all_to_all(back_send, 'blk', split_axis=0, concat_axis=0, tiled=True)]
  transfers between devices with their start and end apart: 3 -> 2, of which waited for: 3 -> 2; matrix products, arithmetic and copies ran while one was open for 3% -> 14% of each run, Pallas kernels for 0% -> 0%
where the time goes in v1:
time: 106 us; the launch traced here: 105 us
  Pallas kernels  47 us (44%)
  local copies, waits for them, and re-layouts  20.2 us (19%)
  starting transfers between devices  15.3 us (14%)
  waiting for transfers between devices  13.8 us (13%)
  matrix products  8.33 us (8%)
    pallas_call x1, Pallas kernels, reduce_both(): pl.pallas_call(functools.partial(reduce_kernel, scale, rings), out_shape=...  47 us
    all_to_all x1, starting transfers between devices, local(): lax.all_to_all(back_send, 'blk', split_axis=0, concat_axis=0, tiled=True)  10 us
    all_to_all x1, waiting for transfers between devices, local(): lax.all_to_all(hidden_send, 'blk', split_axis=0, concat_axis=0, tiled=True)  8.07 us
    all_to_all x1, waiting for transfers between devices, local(): lax.all_to_all(back_send, 'blk', split_axis=0, concat_axis=0, tiled=True)  5.78 us
    unnamed x17, local copies, waits for them, and re-layouts  5.72 us
    all_to_all x1, starting transfers between devices, local(): lax.all_to_all(hidden_send, 'blk', split_axis=0, concat_axis=0, tiled=True)  5.26 us
    dot_general x1, matrix products, local(): jnp.einsum('tci,tbcj->cibj', features, token_major, preferred_element_typ...  3.22 us
    all_to_all x1, local copies, waits for them, and re-layouts, local(): lax.all_to_all(back_send, 'blk', split_axis=0, concat_axis=0, tiled=True)  2.66 us
  transfers between devices with their start and end apart: 2, of which 2 were waited for; matrix products, arithmetic and copies ran while one was open for 14% of the time, Pallas kernels for 0%

profile of v1, /device:TPU:2, one launch (start us, length us, event | category | flops | bytes accessed | tf_op | source)
XLA Modules:
  0.0 105.4 jit_solution(13739894303496319869)
XLA Ops:
  0.6 0.0 copy-start
  0.6 1.7 %copy.64 = bf16[40,8,16,128]{3,2,1,0:T(8,128)(2,1)S(1)} copy(bf16[40,8,16,128]{3,1,2,0:T(8,128)(2,1)} %bitcast.66) | data formatting | bytes 2621440
  2.3 0.0 copy-done
  2.3 0.7 fusion.5
  3.0 0.9 copy.33
  3.9 1.6 %copy.34 = bf16[8,320,256]{2,1,0:T(8,128)(2,1)} copy(bf16[8,320,256]{1,2,0:T(8,128)(2,1)S(1)} %bitcast.53) | data formatting | bytes 2621440 | tf_op jit(solution)/shard_map/reshape | solution.py:158
  5.5 10.0 %all-to-all-start = ((bf16[8,320,256]{2,1,0:T(8,128)(2,1)}), bf16[8,320,256]{2,1,0:T(8,128)(2,1)}, u32[]{:S(2)}, u32[]{:S(2)}) async-start(bf16[8,320,256]{2,1,0:T(8,128)(2,1)} %copy.34), calls=%async_computation | async-start | bytes 2621440 | tf_op jit(solution)/shard_map/all_to_all | solution.py:165
  15.6 1.6 %copy.65 = bf16[40,8,16,128]{3,2,1,0:T(8,128)(2,1)S(1)} copy(bf16[40,8,16,128]{3,1,2,0:T(8,128)(2,1)} %bitcast.67) | data formatting | bytes 2621440
  17.2 0.0 copy-start.1
  17.2 2.4 %copy.36 = bf16[16,128,128]{1,2,0:T(8,128)(2,1)} copy(bf16[16,128,128]{2,1,0:T(8,128)(2,1)} %param.5) | data formatting | bytes 1048576 | tf_op args[1]
  19.6 0.0 copy-done.1
  19.6 1.7 %fusion.6 = bf16[8,320,16,16]{1,3,0,2:T(8,128)(2,1)S(1)} fusion(bf16[16,128,8,16]{1,3,2,0:T(8,128)(2,1)} %bitcast.61, bf16[320,16,128,1]{2,1,0,3:T(8,128)(2,1)S(1)} %bitcast.57), kind=kOutput, calls=%fused_computation.9 | convolution fusion | flops 168427520 | bytes 3145728 | tf_op jit(solution)/shard_map/tci,cibj->btcj/dot_general | solution.py:155
  21.3 0.2 copy.43
  21.5 1.6 %copy.44 = bf16[8,320,256]{2,1,0:T(8,128)(2,1)} copy(bf16[8,320,256]{1,2,0:T(8,128)(2,1)S(1)} %bitcast.54) | data formatting | bytes 2621440 | tf_op jit(solution)/shard_map/reshape | solution.py:156
  23.1 5.8 %all-to-all-done = bf16[8,320,256]{2,1,0:T(8,128)(2,1)} async-done(((bf16[8,320,256]{2,1,0:T(8,128)(2,1)}), bf16[8,320,256]{2,1,0:T(8,128)(2,1)}, u32[]{:S(2)}, u32[]{:S(2)}) %all-to-all-start) | async-done | bytes 1310752 | tf_op jit(solution)/shard_map/all_to_all | solution.py:165
  28.9 5.3 %all-to-all-start.1 = ((bf16[8,320,256]{2,1,0:T(8,128)(2,1)}), bf16[8,320,256]{2,1,0:T(8,128)(2,1)}, u32[]{:S(2)}, u32[]{:S(2)}) async-start(bf16[8,320,256]{2,1,0:T(8,128)(2,1)} %copy.44), calls=%async_computation.1 | async-start | bytes 2621440 | tf_op jit(solution)/shard_map/all_to_all | solution.py:159
  34.1 2.7 %copy.35 = bf16[8,320,256]{1,2,0:T(8,128)(2,1)} copy(bf16[8,320,256]{2,1,0:T(8,128)(2,1)} %all-to-all-done) | data formatting | bytes 2621440 | tf_op jit(solution)/shard_map/all_to_all | solution.py:165
  36.8 0.0 copy-done.2
  36.8 3.2 %fusion = f32[16,8,16,128]{3,2,1,0:T(8,128)} fusion(bf16[8,320,16,16]{1,3,2,0:T(8,128)(2,1)} %bitcast.63, bf16[320,16,128,1]{2,1,0,3:T(8,128)(2,1)S(1)} %bitcast.58), kind=kOutput, calls=%fused_computation.3 | convolution fusion | flops 167772160 | bytes 3670016 | tf_op jit(solution)/shard_map/tci,tbcj->cibj/dot_general | solution.py:173
  40.0 0.0 copy-done.3
  40.0 0.0 copy-done.4
  40.0 1.7 %fusion.7 = bf16[16,40,8,128]{3,2,1,0:T(8,128)(2,1)} fusion(bf16[8,320,16,16]{1,3,2,0:T(8,128)(2,1)S(1)} %bitcast.64, bf16[16,128,8,16]{1,3,2,0:T(8,128)(2,1)S(1)} %bitcast.62), kind=kOutput, calls=%fused_computation.10 | convolution fusion | flops 168427520 | bytes 3145728 | tf_op jit(solution)/shard_map/btcj,cibj->tci/dot_general | solution.py:168
  41.7 8.1 %all-to-all-done.1 = bf16[8,320,256]{2,1,0:T(8,128)(2,1)} async-done(((bf16[8,320,256]{2,1,0:T(8,128)(2,1)}), bf16[8,320,256]{2,1,0:T(8,128)(2,1)}, u32[]{:S(2)}, u32[]{:S(2)}) %all-to-all-start.1) | async-done | bytes 1310752 | tf_op jit(solution)/shard_map/all_to_all | solution.py:159
  49.7 1.8 %copy.45 = bf16[8,320,256]{1,2,0:T(8,128)(2,1)S(1)} copy(bf16[8,320,256]{2,1,0:T(8,128)(2,1)} %all-to-all-done.1) | data formatting | bytes 2621440 | tf_op jit(solution)/shard_map/all_to_all | solution.py:159
  51.6 1.0 fusion.2
  52.6 0.0 copy-start.6
  52.6 1.6 %copy.48 = f32[16,128,128]{2,0,1:T(8,128)} copy(f32[16,128,128]{2,1,0:T(8,128)S(1)} %bitcast.70) | data formatting | bytes 2097152 | tf_op jit(solution)/shard_map/reshape | solution.py:164
  54.2 0.0 copy-done.6
  54.2 1.4 %copy.41 = f32[16,128,128]{2,0,1:T(8,128)} copy(f32[16,128,128]{1,2,0:T(8,128)S(1)} %bitcast.69) | data formatting | bytes 2097152 | tf_op jit(solution)/shard_map/reshape | solution.py:176
  55.6 1.4 %copy.85 = bf16[16,40,8,128]{3,2,0,1:T(8,128)(2,1)} copy(bf16[16,40,8,128]{3,2,1,0:T(8,128)(2,1)S(1)} %copy-done.5) | data formatting | bytes 2621440 | tf_op jit(solution)/shard_map/reshape | solution.py:171
  57.1 47.0 %reduce_over_dp.1 = (f32[32,128]{1,0:T(8,128)}, f32[32,128]{1,0:T(8,128)}) custom-call(f32[16,2,2,32,128]{4,3,2,1,0:T(8,128)} %bitcast.60, f32[16,2,2,32,128]{4,3,2,1,0:T(8,128)} %bitcast.59), custom_call_target="tpu_custom_call" | custom-call | tf_op jit(solution)/shard_map/reduce_over_dp/pallas_call | solution.py:119
  104.1 1.4 %copy_bitcast_fusion.1 = (f32[16,2,128]{2,1,0:T(2,128)}, f32[16,2,128]{2,1,0:T(2,128)}) fusion(f32[2,16,128]{2,1,0:T(8,128)} %bitcast.72, f32[2,16,128]{2,1,0:T(8,128)} %bitcast.71), kind=kLoop, calls=%fused_computation.17 | loop fusion | bytes 65536 | tf_op jit(solution)/shard_map/transpose | solution.py:139
  (5 shorter events, 0.0 us)
Async XLA Ops:
  0.6 1.7 %copy-start = (bf16[16,128,128]{2,1,0:T(8,128)(2,1)S(1)}, bf16[16,128,128]{2,1,0:T(8,128)(2,1)}, u32[]{:S(2)}) copy-start(bf16[16,128,128]{2,1,0:T(8,128)(2,1)} %param.6) | copy-start | bytes 1572868
  5.5 23.3 %all-to-all-start = ((bf16[8,320,256]{2,1,0:T(8,128)(2,1)}), bf16[8,320,256]{2,1,0:T(8,128)(2,1)}, u32[]{:S(2)}, u32[]{:S(2)}) async-start(bf16[8,320,256]{2,1,0:T(8,128)(2,1)} %copy.34), calls=%async_computation | async-start | bytes 2621440 | tf_op jit(solution)/shard_map/all_to_all | solution.py:165
  17.2 2.4 %copy-start.1 = (bf16[40,8,16,128]{3,2,1,0:T(8,128)(2,1)}, bf16[40,8,16,128]{3,2,1,0:T(8,128)(2,1)S(1)}, u32[]{:S(2)}) copy-start(bf16[40,8,16,128]{3,2,1,0:T(8,128)(2,1)S(1)} %copy.65) | copy-start | bytes 3932164
  28.9 20.9 %all-to-all-start.1 = ((bf16[8,320,256]{2,1,0:T(8,128)(2,1)}), bf16[8,320,256]{2,1,0:T(8,128)(2,1)}, u32[]{:S(2)}, u32[]{:S(2)}) async-start(bf16[8,320,256]{2,1,0:T(8,128)(2,1)} %copy.44), calls=%async_computation.1 | async-start | bytes 2621440 | tf_op jit(solution)/shard_map/all_to_all | solution.py:159
  34.1 2.7 %copy-start.2 = (bf16[40,8,16,128]{3,2,1,0:T(8,128)(2,1)S(1)}, bf16[40,8,16,128]{3,2,1,0:T(8,128)(2,1)}, u32[]{:S(2)}) copy-start(bf16[40,8,16,128]{3,2,1,0:T(8,128)(2,1)} %copy-done.1) | copy-start | bytes 3932164
  36.8 3.2 %copy-start.3 = (bf16[16,128,128]{1,2,0:T(8,128)(2,1)S(1)}, bf16[16,128,128]{1,2,0:T(8,128)(2,1)}, u32[]{:S(2)}) copy-start(bf16[16,128,128]{1,2,0:T(8,128)(2,1)} %copy.36) | copy-start | bytes 1572868
  36.8 3.2 %copy-start.4 = (bf16[8,320,256]{1,2,0:T(8,128)(2,1)S(1)}, bf16[8,320,256]{1,2,0:T(8,128)(2,1)}, u32[]{:S(2)}) copy-start(bf16[8,320,256]{1,2,0:T(8,128)(2,1)} %copy.35) | copy-start | bytes 3932164
  52.6 1.6 %copy-start.6 = (f32[16,8,16,128]{3,2,1,0:T(8,128)S(1)}, f32[16,8,16,128]{3,2,1,0:T(8,128)}, u32[]{:S(2)}) copy-start(f32[16,8,16,128]{3,2,1,0:T(8,128)} %fusion) | copy-start | bytes 3145732
  54.2 1.4 %copy-start.5 = (bf16[16,40,8,128]{3,2,1,0:T(8,128)(2,1)S(1)}, bf16[16,40,8,128]{3,2,1,0:T(8,128)(2,1)}, u32[]{:S(2)}) copy-start(bf16[16,40,8,128]{3,2,1,0:T(8,128)(2,1)} %fusion.7) | copy-start | bytes 3932164

commit v2 on v0

v2 whole, which is shorter than its diff:
```python
import functools

import jax
import jax.numpy as jnp
from jax import lax
from jax.experimental import pallas as pl
from jax.experimental.pallas import tpu as pltpu
from jax.sharding import PartitionSpec as P

MESH = pl.DeviceIdType.MESH
OFFSETS = ((2, 1), (2, 0), (1, 1), (3, 1), (1, 0), (3, 0), (0, 1))
NN = (((1,), (0,)), ((), ()))
NT = (((1,), (1,)), ((), ()))
TN = (((0,), (0,)), ((), ()))


def dot(a, b, dims):
    return lax.dot_general(a, b, dims, preferred_element_type=jnp.float32)


def swapped(index):
    return (index & ~6) | ((index & 4) >> 1) | ((index & 2) << 1)


def one_hot(rows, pick):
    row = lax.broadcasted_iota(jnp.int32, (rows, rows), 0)
    col = lax.broadcasted_iota(jnp.int32, (rows, rows), 1)
    return jnp.where(col == pick(row), 1.0, 0.0).astype(jnp.bfloat16)


def monarch_kernel(
    scale, rings, x_ref, l_ref, r_ref, g_ref, gin_ref, lo_ref, ro_ref,
    hc, hs, hr, bc, bs, br, xt, lt, sr, sl, pair, up, down, fold,
    hid_s, hid_r, back_s, back_r,
    pair_s, pair_r, up_s, up_r, down_s, down_r, fold_s, fold_r,
):
    owned, width = l_ref.shape[0], l_ref.shape[1]
    tokens = x_ref.shape[0]
    me = lax.axis_index("dp")
    core, high, z = lax.rem(me, 2), lax.rem(me // 2, 2), me // 4
    half = rings // 2
    mate = me + 1 - 2 * core
    across = me + 2 - 4 * high
    above = lax.rem(z + 1, rings) * 4 + high * 2 + core
    below = lax.rem(z + rings - 1, rings) * 4 + high * 2 + core
    blk = lax.axis_index("blk")
    blk_y, blk_x = blk // 4, lax.rem(blk, 4)
    partners = [
        lax.rem(blk_y + dy, 2) * 4 + lax.rem(blk_x + dx, 4) for dx, dy in OFFSETS
    ]

    barrier = pltpu.get_barrier_semaphore()
    for peer in (mate, across, above, below):
        pl.semaphore_signal(barrier, inc=1, device_id={"dp": peer}, device_id_type=MESH)
    for peer in partners:
        pl.semaphore_signal(barrier, inc=1, device_id={"blk": peer}, device_id_type=MESH)

    def send(src, dst, send_sem, recv_sem, axis, peer):
        copy = pltpu.make_async_remote_copy(
            src_ref=src, dst_ref=dst, send_sem=send_sem, recv_sem=recv_sem,
            device_id={axis: peer}, device_id_type=MESH,
        )
        copy.start()
        return copy

    def columns(c):
        return pl.ds(pl.multiple_of(c * width, width), width)

    def split(value):
        return value.astype(jnp.bfloat16).reshape(width // owned, owned, tokens)

    def hidden_block(c, carry):
        lt[c] = l_ref[c].T
        hc[:, c] = split(dot(lt[c], x_ref[:, columns(c)], NT))
        return carry

    def back_block(j, carry):
        bc[:, j] = split(dot(r_ref[j], g_ref[:, columns(j)], NT))
        return carry

    def exchange(blocks, staged, landed, order, send_sem, recv_sem):
        copies = []
        for n, peer in enumerate((*partners, blk)):
            rows = blocks[peer].reshape(owned * owned, tokens)
            moved = dot(order, rows, NN).astype(jnp.bfloat16).reshape(owned, owned, tokens)
            if n < len(partners):
                staged[n] = moved
                copies.append(
                    send(staged.at[n], landed.at[:, blk], send_sem.at[n], recv_sem.at[n], "blk", peer)
                )
            else:
                landed[:, blk] = moved
        return copies

    lax.fori_loop(0, owned, hidden_block, 0, unroll=2)
    to_right = one_hot(owned * owned, lambda r: (swapped(r & 15) << 4) | (r >> 4))
    pl.semaphore_wait(barrier, 4 + len(partners))
    hidden_copies = exchange(hc, hs, hr, to_right, hid_s, hid_r)
    lax.fori_loop(0, owned, back_block, 0, unroll=2)
    to_left = one_hot(owned * owned, lambda r: ((r & 15) << 4) | (r >> 4))
    back_copies = exchange(bc, bs, br, to_left, back_s, back_r)

    turn = one_hot(width, swapped)

    def turn_block(c, carry):
        xt[c] = dot(turn, x_ref[:, columns(c)], NT).astype(jnp.bfloat16)
        return carry

    lax.fori_loop(0, owned, turn_block, 0, unroll=2)

    order = []
    for step in range(half):
        order.append(lax.rem(z + half - step, rings))
        if step < half - 1:
            order.append(lax.rem(z + rings - (half - 1 - step), rings))
    order.append(z)
    piece = owned * 4

    def reduce_lane(lane, ref, out, between):
        def part(target, which):
            return pl.ds(pl.multiple_of(target * (2 * piece) + which * piece, piece), piece)

        pairs = [
            send(
                ref.at[part(target, 1 - core)], pair.at[lane, k],
                pair_s.at[lane, k], pair_r.at[lane, k], "dp", mate,
            )
            for k, target in enumerate(order)
        ]
        started = list(pairs)

        def own(k):
            pairs[k].wait_recv()
            return pair[lane, k] + ref[part(order[k], core)]

        def advance(step, k, before, held, send_sem, recv_sem, peer):
            mine = own(k)
            if step == 0:
                source = pair.at[lane, k]
                source[...] = mine
            else:
                before.wait_recv()
                source = held.at[lane, step - 1]
                source[...] += mine
            copy = send(
                source, held.at[lane, step], send_sem.at[lane, step], recv_sem.at[lane, step], "dp", peer
            )
            started.append(copy)
            return copy

        rise = sink = None
        for step in range(half):
            rise = advance(step, 2 * step, rise, up, up_s, up_r, above)
            if step < half - 1:
                sink = advance(step, 2 * step + 1, sink, down, down_s, down_r, below)
            between(step)
        mine = own(rings - 1)
        rise.wait_recv()
        sink.wait_recv()
        last = pair.at[lane, rings - 1]
        last[...] = mine + up[lane, half - 1] + down[lane, half - 2]

        def part_of(which):
            return pl.ds(pl.multiple_of(which * (piece // 2), piece // 2), piece // 2)

        folded = send(
            last.at[part_of(1 - high)], fold.at[lane], fold_s.at[lane], fold_r.at[lane], "dp", across
        )
        started.append(folded)

        def finish():
            folded.wait_recv()
            out[...] = (last[part_of(high)] + fold[lane]) * scale
            for copy in started:
                copy.wait_send()

        return finish

    for copy in hidden_copies:
        copy.wait_recv()
    for j in range(owned):
        sr[pl.ds(j, width, stride=owned), :] = dot(
            hr[j].reshape(width, tokens), g_ref[:, j * width:(j + 1) * width], NN
        )
    finish_right = reduce_lane(0, sr, ro_ref, lambda step: None)

    for copy in back_copies:
        copy.wait_recv()
    for c in range(owned):
        sl[pl.ds(c, width, stride=owned), :] = dot(xt[c], br[c].reshape(width, tokens), NT)

    def grad_in(step):
        for c in range(2 * step, 2 * step + 2):
            gin_ref[:, c * width:(c + 1) * width] = dot(
                br[c].reshape(width, tokens), lt[c], TN
            ).astype(jnp.bfloat16)

    finish_left = reduce_lane(1, sl, lo_ref, grad_in)
    finish_right()
    finish_left()
    for copy in (*hidden_copies, *back_copies):
        copy.wait_send()


def local(inputs, left_factor, right_factor, grad_output):
    replicas = lax.axis_size("dp")
    groups = lax.axis_size("blk")
    tokens = inputs.shape[0]
    owned, width = left_factor.shape[0], left_factor.shape[1]
    scale = float(tokens * replicas) ** (-0.5)
    rings = replicas // 4
    half = rings // 2
    rows = owned * (width // replicas)
    dma = pltpu.SemaphoreType.DMA
    vmem = pl.BlockSpec(memory_space=pltpu.VMEM)
    bf16, f32 = jnp.bfloat16, jnp.float32
    grad, left, right = pl.pallas_call(
        functools.partial(monarch_kernel, scale, rings),
        out_shape=[
            jax.ShapeDtypeStruct(inputs.shape, bf16),
            jax.ShapeDtypeStruct((rows, width), f32),
            jax.ShapeDtypeStruct((rows, width), f32),
        ],
        in_specs=[vmem] * 4,
        out_specs=[vmem] * 3,
        scratch_shapes=[
            pltpu.VMEM((groups, owned, owned, tokens), bf16),
            pltpu.VMEM((groups - 1, owned, owned, tokens), bf16),
            pltpu.VMEM((owned, groups, owned, tokens), bf16),
            pltpu.VMEM((groups, owned, owned, tokens), bf16),
            pltpu.VMEM((groups - 1, owned, owned, tokens), bf16),
            pltpu.VMEM((owned, groups, owned, tokens), bf16),
            pltpu.VMEM((owned, width, tokens), bf16),
            pltpu.VMEM((owned, width, width), bf16),
            pltpu.VMEM((owned * width, width), f32),
            pltpu.VMEM((owned * width, width), f32),
            pltpu.VMEM((2, rings, 2 * rows, width), f32),
            pltpu.VMEM((2, half, 2 * rows, width), f32),
            pltpu.VMEM((2, half - 1, 2 * rows, width), f32),
            pltpu.VMEM((2, rows, width), f32),
            dma((groups - 1,)), dma((groups - 1,)), dma((groups - 1,)), dma((groups - 1,)),
            dma((2, rings)), dma((2, rings)),
            dma((2, half)), dma((2, half)),
            dma((2, half - 1)), dma((2, half - 1)),
            dma((2,)), dma((2,)),
        ],
        compiler_params=pltpu.CompilerParams(
            collective_id=0, has_side_effects=True, vmem_limit_bytes=58 * 1024 * 1024
        ),
        name="monarch_backward",
    )(inputs, left_factor, right_factor, grad_output)

    def restore(out):
        return jnp.transpose(out.reshape(width // replicas, owned, width), (1, 0, 2))

    return grad, restore(left), restore(right)


def solution(mesh):
    return jax.shard_map(
        local,
        mesh=mesh,
        in_specs=(P("dp", "blk"), P("blk", None, None), P("blk", None, None), P("dp", "blk")),
        out_specs=(P("dp", "blk"), P("blk", "dp", None), P("blk", "dp", None)),
        check_vma=False,
    )
```

time: 480 us -> 107 us (0.22)
  waiting for transfers between devices: 406 us -> 0 us
  Pallas kernels: 0 us -> 102 us
  blocking collectives: 20.5 us -> 0 us
  local copies, waits for them, and re-layouts: 21.2 us -> 3.88 us
  between operations: 14.2 us -> 0.64 us
  starting transfers between devices: 10.1 us -> 0 us
  matrix products: 7.53 us -> 0 us
    reduce_scatter x2 -> x0, waiting for transfers between devices: 394 us -> none  [the longest x1 213 us: local(): lax.psum_scatter(left_term, 'dp', scatter_dimension=1, tiled=True)]
    pallas_call x0 -> x1, Pallas kernels: none -> 102 us  [local(): pl.pallas_call(functools.partial(monarch_kernel, scale, rings), out_shape...]
    all_to_all x1 -> x0, blocking collectives: 20.5 us -> none  [local(): lax.all_to_all(back_send, 'blk', split_axis=0, concat_axis=0, tiled=True)]
    all_to_all x1 -> x0, waiting for transfers between devices: 11.7 us -> none  [local(): lax.all_to_all(hidden_send, 'blk', split_axis=0, concat_axis=0, tiled=True)]
    all_to_all x1 -> x0, starting transfers between devices: 10 us -> none  [local(): lax.all_to_all(hidden_send, 'blk', split_axis=0, concat_axis=0, tiled=True)]
    dot_general x5 -> x0, matrix products: 7.53 us -> none  [the longest x1 3.11 us: local(): jnp.einsum('tci,tbcj->cibj', features, token_major, preferred_element_typ...]
  transfers between devices with their start and end apart: 3 -> 0, of which waited for: 3 -> 0; matrix products, arithmetic and copies ran while one was open for 3% -> 0% of each run, Pallas kernels for 0% -> 0%
where the time goes in v2:
time: 107 us; the launch traced here: 106 us
  Pallas kernels  102 us (95%)
  local copies, waits for them, and re-layouts  3.88 us (4%)
    pallas_call x1, Pallas kernels, local(): pl.pallas_call(functools.partial(monarch_kernel, scale, rings), out_shape...  102 us
    unnamed x1, local copies, waits for them, and re-layouts  2.52 us

profile of v2, /device:TPU:2, one launch (start us, length us, event | category | flops | bytes accessed | tf_op | source)
XLA Modules:
  0.0 106.4 jit_solution(14220372966066226925)
XLA Ops:
  0.6 101.9 %monarch_backward.1 = (bf16[320,2048]{1,0:T(8,128)(2,1)}, f32[32,128]{1,0:T(8,128)}, f32[32,128]{1,0:T(8,128)}) custom-call(bf16[320,2048]{1,0:T(8,128)(2,1)} %x_ref.1, bf16[16,128,128]{2,1,0:T(8,128)(2,1)} %l_ref.1, bf16[16,128,128]{2,1,0:T(8,128)(2,1)} %r_ref.1, bf16[320,2048]{1,0:T(8,128)(2,1)} %g_ref.1), custom_call_target="tpu_custom_call" | custom-call | tf_op jit(solution)/shard_map/monarch_backward/pallas_call | solution.py:217
  102.5 1.4 %copy_bitcast_fusion = (f32[16,2,128]{2,1,0:T(2,128)}, f32[16,2,128]{2,1,0:T(2,128)}) fusion(f32[2,16,128]{2,1,0:T(8,128)} %bitcast.7, f32[2,16,128]{2,1,0:T(8,128)} %bitcast.6), kind=kLoop, calls=%fused_computation | loop fusion | bytes 65536 | tf_op jit(solution)/shard_map/transpose | solution.py:254
  103.9 2.5 %copy.12 = bf16[320,2048]{1,0:T(8,128)(2,1)} copy(bf16[320,2048]{1,0:T(8,128)(2,1)} %get-tuple-element.14) | data formatting | bytes 2621440

commit v3 on v2

--- a/solution.py
+++ b/solution.py
@@ -9,6 +9,7 @@
 
 MESH = pl.DeviceIdType.MESH
 OFFSETS = ((2, 1), (2, 0), (1, 1), (3, 1), (1, 0), (3, 0), (0, 1))
+LEAD = 5
 NN = (((1,), (0,)), ((), ()))
 NT = (((1,), (1,)), ((), ()))
 TN = (((0,), (0,)), ((), ()))
@@ -116,65 +117,67 @@
     order.append(z)
     piece = owned * 4
 
-    def reduce_lane(lane, ref, out, between):
-        def part(target, which):
-            return pl.ds(pl.multiple_of(target * (2 * piece) + which * piece, piece), piece)
-
+    halves = (1 - high, high)
+    slab = piece // 2
+
+    def rows_at(start, count):
+        return pl.ds(pl.multiple_of(start, count), count)
+
+    def reduce_lane(lane, ref, out):
         pairs = [
             send(
-                ref.at[part(target, 1 - core)], pair.at[lane, k],
+                ref.at[rows_at(target * (2 * piece) + (1 - core) * piece, piece)], pair.at[lane, k],
                 pair_s.at[lane, k], pair_r.at[lane, k], "dp", mate,
             )
             for k, target in enumerate(order)
         ]
         started = list(pairs)
 
-        def own(k):
-            pairs[k].wait_recv()
-            return pair[lane, k] + ref[part(order[k], core)]
-
-        def advance(step, k, before, held, send_sem, recv_sem, peer):
-            mine = own(k)
+        def own(k, e):
+            if e == 0:
+                pairs[k].wait_recv()
+            start = order[k] * (2 * piece) + core * piece + halves[e] * slab
+            return pair[lane, k, rows_at(halves[e] * slab, slab)] + ref[rows_at(start, slab)]
+
+        def advance(step, k, e, before, held, send_sem, recv_sem, peer):
+            mine = own(k, e)
             if step == 0:
-                source = pair.at[lane, k]
+                source = pair.at[lane, k, rows_at(halves[e] * slab, slab)]
                 source[...] = mine
             else:
                 before.wait_recv()
-                source = held.at[lane, step - 1]
+                source = held.at[lane, e, step - 1]
                 source[...] += mine
             copy = send(
-                source, held.at[lane, step], send_sem.at[lane, step], recv_sem.at[lane, step], "dp", peer
+                source, held.at[lane, e, step],
+                send_sem.at[lane, e, step], recv_sem.at[lane, e, step], "dp", peer,
             )
             started.append(copy)
             return copy
 
-        rise = sink = None
+        rise, sink = [None, None], [None, None]
         for step in range(half):
-            rise = advance(step, 2 * step, rise, up, up_s, up_r, above)
-            if step < half - 1:
-                sink = advance(step, 2 * step + 1, sink, down, down_s, down_r, below)
-            between(step)
-        mine = own(rings - 1)
-        rise.wait_recv()
-        sink.wait_recv()
+            for e in range(2):
+                rise[e] = advance(step, 2 * step, e, rise[e], up, up_s, up_r, above)
+                if step < half - 1:
+                    sink[e] = advance(step, 2 * step + 1, e, sink[e], down, down_s, down_r, below)
+            yield
         last = pair.at[lane, rings - 1]
-        last[...] = mine + up[lane, half - 1] + down[lane, half - 2]
-
-        def part_of(which):
-            return pl.ds(pl.multiple_of(which * (piece // 2), piece // 2), piece // 2)
-
-        folded = send(
-            last.at[part_of(1 - high)], fold.at[lane], fold_s.at[lane], fold_r.at[lane], "dp", across
-        )
-        started.append(folded)
-
-        def finish():
-            folded.wait_recv()
-            out[...] = (last[part_of(high)] + fold[lane]) * scale
-            for copy in started:
-                copy.wait_send()
-
-        return finish
+        for e in range(2):
+            mine = own(rings - 1, e)
+            rise[e].wait_recv()
+            sink[e].wait_recv()
+            total = last.at[rows_at(halves[e] * slab, slab)]
+            total[...] = mine + up[lane, e, half - 1] + down[lane, e, half - 2]
+            if e == 0:
+                folded = send(total, fold.at[lane], fold_s.at[lane], fold_r.at[lane], "dp", across)
+                started.append(folded)
+        yield
+        folded.wait_recv()
+        out[...] = (last[rows_at(high * slab, slab)] + fold[lane]) * scale
+        for copy in started:
+            copy.wait_send()
+        yield
 
     for copy in hidden_copies:
         copy.wait_recv()
@@ -182,7 +185,9 @@
         sr[pl.ds(j, width, stride=owned), :] = dot(
             hr[j].reshape(width, tokens), g_ref[:, j * width:(j + 1) * width], NN
         )
-    finish_right = reduce_lane(0, sr, ro_ref, lambda step: None)
+    right_lane = reduce_lane(0, sr, ro_ref)
+    for _ in range(LEAD):
+        next(right_lane)
 
     for copy in back_copies:
         copy.wait_recv()
@@ -195,9 +200,13 @@
                 br[c].reshape(width, tokens), lt[c], TN
             ).astype(jnp.bfloat16)
 
-    finish_left = reduce_lane(1, sl, lo_ref, grad_in)
-    finish_right()
-    finish_left()
+    left_lane = reduce_lane(1, sl, lo_ref)
+    for step in range(half + 2):
+        if step + LEAD < half + 2:
+            next(right_lane)
+        next(left_lane)
+        if step < half:
+            grad_in(step)
     for copy in (*hidden_copies, *back_copies):
         copy.wait_send()
 
@@ -235,13 +244,13 @@
             pltpu.VMEM((owned * width, width), f32),
             pltpu.VMEM((owned * width, width), f32),
             pltpu.VMEM((2, rings, 2 * rows, width), f32),
-            pltpu.VMEM((2, half, 2 * rows, width), f32),
-            pltpu.VMEM((2, half - 1, 2 * rows, width), f32),
+            pltpu.VMEM((2, 2, half, rows, width), f32),
+            pltpu.VMEM((2, 2, half - 1, rows, width), f32),
             pltpu.VMEM((2, rows, width), f32),
             dma((groups - 1,)), dma((groups - 1,)), dma((groups - 1,)), dma((groups - 1,)),
             dma((2, rings)), dma((2, rings)),
-            dma((2, half)), dma((2, half)),
-            dma((2, half - 1)), dma((2, half - 1)),
+            dma((2, 2, half)), dma((2, 2, half)),
+            dma((2, 2, half - 1)), dma((2, 2, half - 1)),
             dma((2,)), dma((2,)),
         ],
         compiler_params=pltpu.CompilerParams(

time: 107 us -> 97.4 us (0.910)
  Pallas kernels: 102 us -> 92.5 us
    pallas_call x1, Pallas kernels: 102 us -> 92.5 us  [local(): pl.pallas_call(functools.partial(monarch_kernel, scale, rings), out_shape...]
where the time goes in v3:
time: 97.4 us; the launch traced here: 97 us
  Pallas kernels  92.5 us (95%)
  local copies, waits for them, and re-layouts  3.88 us (4%)
    pallas_call x1, Pallas kernels, local(): pl.pallas_call(functools.partial(monarch_kernel, scale, rings), out_shape...  92.5 us
    unnamed x1, local copies, waits for them, and re-layouts  2.52 us

profile of v3, /device:TPU:2, one launch (start us, length us, event | category | flops | bytes accessed | tf_op | source)
XLA Modules:
  0.0 97.0 jit_solution(3771582849903243392)
XLA Ops:
  0.6 92.5 %monarch_backward.1 = (bf16[320,2048]{1,0:T(8,128)(2,1)}, f32[32,128]{1,0:T(8,128)}, f32[32,128]{1,0:T(8,128)}) custom-call(bf16[320,2048]{1,0:T(8,128)(2,1)} %x_ref.1, bf16[16,128,128]{2,1,0:T(8,128)(2,1)} %l_ref.1, bf16[16,128,128]{2,1,0:T(8,128)(2,1)} %r_ref.1, bf16[320,2048]{1,0:T(8,128)(2,1)} %g_ref.1), custom_call_target="tpu_custom_call" | custom-call | tf_op jit(solution)/shard_map/monarch_backward/pallas_call | solution.py:226
  93.2 1.4 %copy_bitcast_fusion = (f32[16,2,128]{2,1,0:T(2,128)}, f32[16,2,128]{2,1,0:T(2,128)}) fusion(f32[2,16,128]{2,1,0:T(8,128)} %bitcast.7, f32[2,16,128]{2,1,0:T(8,128)} %bitcast.6), kind=kLoop, calls=%fused_computation | loop fusion | bytes 65536 | tf_op jit(solution)/shard_map/transpose | solution.py:263
  94.5 2.5 %copy.12 = bf16[320,2048]{1,0:T(8,128)(2,1)} copy(bf16[320,2048]{1,0:T(8,128)(2,1)} %get-tuple-element.14) | data formatting | bytes 2621440

commit v4 on v3

--- a/solution.py
+++ b/solution.py
@@ -31,12 +31,14 @@
 
 def monarch_kernel(
     scale, rings, x_ref, l_ref, r_ref, g_ref, gin_ref, lo_ref, ro_ref,
-    hc, hs, hr, bc, bs, br, xt, lt, sr, sl, pair, up, down, fold,
+    hc, hs, hs_end, hr, hr_end, bc, bs, bs_end, br, br_end, xt, lt, sr, sl, pair, up, down, fold,
     hid_s, hid_r, back_s, back_r,
     pair_s, pair_r, up_s, up_r, down_s, down_r, fold_s, fold_r,
 ):
     owned, width = l_ref.shape[0], l_ref.shape[1]
     tokens = x_ref.shape[0]
+    body = hr.shape[-1]
+    rest = tokens - body
     me = lax.axis_index("dp")
     core, high, z = lax.rem(me, 2), lax.rem(me // 2, 2), me // 4
     half = rings // 2
@@ -83,31 +85,47 @@
         copies = []
         for n, peer in enumerate((*partners, blk)):
             rows = blocks[peer].reshape(owned * owned, tokens)
-            moved = dot(order, rows, NN).astype(jnp.bfloat16).reshape(owned, owned, tokens)
-            if n < len(partners):
-                staged[n] = moved
-                copies.append(
-                    send(staged.at[n], landed.at[:, blk], send_sem.at[n], recv_sem.at[n], "blk", peer)
-                )
-            else:
-                landed[:, blk] = moved
+            moved = dot(order, rows, NN)
+            ends = jnp.concatenate([moved[:width, body:], moved[width:, body:]], axis=1)
+            pieces = (
+                moved[:, :body].astype(jnp.bfloat16).reshape(owned, owned, body),
+                ends.astype(jnp.bfloat16).reshape(owned // 2, owned, 2 * rest),
+            )
+            for part, value in enumerate(pieces):
+                if n < len(partners):
+                    staged[part][n] = value
+                    copies.append(
+                        send(
+                            staged[part].at[n], landed[part].at[:, blk],
+                            send_sem.at[part, n], recv_sem.at[part, n], "blk", peer,
+                        )
+                    )
+                else:
+                    landed[part][:, blk] = value
         return copies
+
+    def spread(value, block):
+        blank = jnp.zeros_like(value)
+        return jnp.concatenate([value, blank] if block < owned // 2 else [blank, value], axis=0)
 
     lax.fori_loop(0, owned, hidden_block, 0, unroll=2)
     to_right = one_hot(owned * owned, lambda r: (swapped(r & 15) << 4) | (r >> 4))
     pl.semaphore_wait(barrier, 4 + len(partners))
-    hidden_copies = exchange(hc, hs, hr, to_right, hid_s, hid_r)
+    hidden_copies = exchange(hc, (hs, hs_end), (hr, hr_end), to_right, hid_s, hid_r)
     lax.fori_loop(0, owned, back_block, 0, unroll=2)
     to_left = one_hot(owned * owned, lambda r: ((r & 15) << 4) | (r >> 4))
-    back_copies = exchange(bc, bs, br, to_left, back_s, back_r)
+    back_copies = exchange(bc, (bs, bs_end), (br, br_end), to_left, back_s, back_r)
 
     turn = one_hot(width, swapped)
 
-    def turn_block(c, carry):
-        xt[c] = dot(turn, x_ref[:, columns(c)], NT).astype(jnp.bfloat16)
+    def turn_block(n, carry):
+        for first in (0, owned // 2):
+            c = n + first
+            rows = jnp.concatenate([x_ref[:body, columns(c)], spread(x_ref[body:, columns(c)], first)], axis=0)
+            xt[c] = dot(turn, rows, NT).astype(jnp.bfloat16)
         return carry
 
-    lax.fori_loop(0, owned, turn_block, 0, unroll=2)
+    lax.fori_loop(0, owned // 2, turn_block, 0)
 
     order = []
     for step in range(half):
@@ -182,9 +200,11 @@
     for copy in hidden_copies:
         copy.wait_recv()
     for j in range(owned):
+        across_j = slice(j * width, (j + 1) * width)
+        ends = hr_end[j % (owned // 2)].reshape(width, 2 * rest)
         sr[pl.ds(j, width, stride=owned), :] = dot(
-            hr[j].reshape(width, tokens), g_ref[:, j * width:(j + 1) * width], NN
-        )
+            hr[j].reshape(width, body), g_ref[:body, across_j], NN
+        ) + dot(ends, spread(g_ref[body:, across_j], j), NN)
     right_lane = reduce_lane(0, sr, ro_ref)
     for _ in range(LEAD):
         next(right_lane)
@@ -192,13 +212,18 @@
     for copy in back_copies:
         copy.wait_recv()
     for c in range(owned):
-        sl[pl.ds(c, width, stride=owned), :] = dot(xt[c], br[c].reshape(width, tokens), NT)
+        ends = br_end[c % (owned // 2)].reshape(width, 2 * rest)
+        sl[pl.ds(c, width, stride=owned), :] = dot(
+            xt[c, :, :body], br[c].reshape(width, body), NT
+        ) + dot(xt[c, :, body:], ends, NT)
 
     def grad_in(step):
         for c in range(2 * step, 2 * step + 2):
-            gin_ref[:, c * width:(c + 1) * width] = dot(
-                br[c].reshape(width, tokens), lt[c], TN
-            ).astype(jnp.bfloat16)
+            across_c = slice(c * width, (c + 1) * width)
+            gin_ref[:body, across_c] = dot(br[c].reshape(width, body), lt[c], TN).astype(jnp.bfloat16)
+            ends = dot(br_end[c % (owned // 2)].reshape(width, 2 * rest), lt[c], TN)
+            first = c // (owned // 2) * rest
+            gin_ref[body:, across_c] = ends[first:first + rest].astype(jnp.bfloat16)
 
     left_lane = reduce_lane(1, sl, lo_ref)
     for step in range(half + 2):
@@ -219,6 +244,7 @@
     scale = float(tokens * replicas) ** (-0.5)
     rings = replicas // 4
     half = rings // 2
+    body = tokens - width // 2
     rows = owned * (width // replicas)
     dma = pltpu.SemaphoreType.DMA
     vmem = pl.BlockSpec(memory_space=pltpu.VMEM)
@@ -234,12 +260,16 @@
         out_specs=[vmem] * 3,
         scratch_shapes=[
             pltpu.VMEM((groups, owned, owned, tokens), bf16),
-            pltpu.VMEM((groups - 1, owned, owned, tokens), bf16),
-            pltpu.VMEM((owned, groups, owned, tokens), bf16),
+            pltpu.VMEM((groups - 1, owned, owned, body), bf16),
+            pltpu.VMEM((groups - 1, owned // 2, owned, width), bf16),
+            pltpu.VMEM((owned, groups, owned, body), bf16),
+            pltpu.VMEM((owned // 2, groups, owned, width), bf16),
             pltpu.VMEM((groups, owned, owned, tokens), bf16),
-            pltpu.VMEM((groups - 1, owned, owned, tokens), bf16),
-            pltpu.VMEM((owned, groups, owned, tokens), bf16),
-            pltpu.VMEM((owned, width, tokens), bf16),
+            pltpu.VMEM((groups - 1, owned, owned, body), bf16),
+            pltpu.VMEM((groups - 1, owned // 2, owned, width), bf16),
+            pltpu.VMEM((owned, groups, owned, body), bf16),
+            pltpu.VMEM((owned // 2, groups, owned, width), bf16),
+            pltpu.VMEM((owned, width, body + width), bf16),
             pltpu.VMEM((owned, width, width), bf16),
             pltpu.VMEM((owned * width, width), f32),
             pltpu.VMEM((owned * width, width), f32),
@@ -247,7 +277,7 @@
             pltpu.VMEM((2, 2, half, rows, width), f32),
             pltpu.VMEM((2, 2, half - 1, rows, width), f32),
             pltpu.VMEM((2, rows, width), f32),
-            dma((groups - 1,)), dma((groups - 1,)), dma((groups - 1,)), dma((groups - 1,)),
+            *[dma((2, groups - 1))] * 4,
             dma((2, rings)), dma((2, rings)),
             dma((2, 2, half)), dma((2, 2, half)),
             dma((2, 2, half - 1)), dma((2, 2, half - 1)),

time: 97.4 us -> 92.8 us (0.953)
  Pallas kernels: 92.5 us -> 88 us
    pallas_call x1, Pallas kernels: 92.5 us -> 88 us  [local(): pl.pallas_call(functools.partial(monarch_kernel, scale, rings), out_shape...]
where the time goes in v4:
time: 92.8 us; the launch traced here: 92.5 us
  Pallas kernels  88 us (95%)
  local copies, waits for them, and re-layouts  3.88 us (4%)
    pallas_call x1, Pallas kernels, local(): pl.pallas_call(functools.partial(monarch_kernel, scale, rings), out_shape...  88 us
    unnamed x1, local copies, waits for them, and re-layouts  2.52 us

profile of v4, /device:TPU:2, one launch (start us, length us, event | category | flops | bytes accessed | tf_op | source)
XLA Modules:
  0.0 92.5 jit_solution(15453318739435397060)
XLA Ops:
  0.6 88.0 %monarch_backward.1 = (bf16[320,2048]{1,0:T(8,128)(2,1)}, f32[32,128]{1,0:T(8,128)}, f32[32,128]{1,0:T(8,128)}) custom-call(bf16[320,2048]{1,0:T(8,128)(2,1)} %x_ref.1, bf16[16,128,128]{2,1,0:T(8,128)(2,1)} %l_ref.1, bf16[16,128,128]{2,1,0:T(8,128)(2,1)} %r_ref.1, bf16[320,2048]{1,0:T(8,128)(2,1)} %g_ref.1), custom_call_target="tpu_custom_call" | custom-call | tf_op jit(solution)/shard_map/monarch_backward/pallas_call | solution.py:252
  88.6 1.4 %copy_bitcast_fusion = (f32[16,2,128]{2,1,0:T(2,128)}, f32[16,2,128]{2,1,0:T(2,128)}) fusion(f32[2,16,128]{2,1,0:T(8,128)} %bitcast.7, f32[2,16,128]{2,1,0:T(8,128)} %bitcast.6), kind=kLoop, calls=%fused_computation | loop fusion | bytes 65536 | tf_op jit(solution)/shard_map/transpose | solution.py:293
  90.0 2.5 %copy.12 = bf16[320,2048]{1,0:T(8,128)(2,1)} copy(bf16[320,2048]{1,0:T(8,128)(2,1)} %get-tuple-element.14) | data formatting | bytes 2621440

commit v5 on v4

--- a/solution.py
+++ b/solution.py
@@ -9,7 +9,7 @@
 
 MESH = pl.DeviceIdType.MESH
 OFFSETS = ((2, 1), (2, 0), (1, 1), (3, 1), (1, 0), (3, 0), (0, 1))
-LEAD = 5
+LEAD = 2
 NN = (((1,), (0,)), ((), ()))
 NT = (((1,), (1,)), ((), ()))
 TN = (((0,), (0,)), ((), ()))

time: 92.8 us -> 87.1 us (0.939)
  Pallas kernels: 88 us -> 82.3 us
    pallas_call x1, Pallas kernels: 88 us -> 82.3 us  [local(): pl.pallas_call(functools.partial(monarch_kernel, scale, rings), out_shape...]
where the time goes in v5:
time: 87.1 us; the launch traced here: 86.8 us
  Pallas kernels  82.3 us (94%)
  local copies, waits for them, and re-layouts  3.88 us (4%)
    pallas_call x1, Pallas kernels, local(): pl.pallas_call(functools.partial(monarch_kernel, scale, rings), out_shape...  82.3 us
    unnamed x1, local copies, waits for them, and re-layouts  2.52 us

profile of v5, /device:TPU:2, one launch (start us, length us, event | category | flops | bytes accessed | tf_op | source)
XLA Modules:
  0.0 86.8 jit_solution(13444635560718552338)
XLA Ops:
  0.6 82.3 %monarch_backward.1 = (bf16[320,2048]{1,0:T(8,128)(2,1)}, f32[32,128]{1,0:T(8,128)}, f32[32,128]{1,0:T(8,128)}) custom-call(bf16[320,2048]{1,0:T(8,128)(2,1)} %x_ref.1, bf16[16,128,128]{2,1,0:T(8,128)(2,1)} %l_ref.1, bf16[16,128,128]{2,1,0:T(8,128)(2,1)} %r_ref.1, bf16[320,2048]{1,0:T(8,128)(2,1)} %g_ref.1), custom_call_target="tpu_custom_call" | custom-call | tf_op jit(solution)/shard_map/monarch_backward/pallas_call | solution.py:252
  82.9 1.4 %copy_bitcast_fusion = (f32[16,2,128]{2,1,0:T(2,128)}, f32[16,2,128]{2,1,0:T(2,128)}) fusion(f32[2,16,128]{2,1,0:T(8,128)} %bitcast.7, f32[2,16,128]{2,1,0:T(8,128)} %bitcast.6), kind=kLoop, calls=%fused_computation | loop fusion | bytes 65536 | tf_op jit(solution)/shard_map/transpose | solution.py:293
  84.3 2.5 %copy.12 = bf16[320,2048]{1,0:T(8,128)(2,1)} copy(bf16[320,2048]{1,0:T(8,128)(2,1)} %get-tuple-element.14) | data formatting | bytes 2621440

commit v6 on v5

--- a/solution.py
+++ b/solution.py
@@ -108,11 +108,11 @@
         blank = jnp.zeros_like(value)
         return jnp.concatenate([value, blank] if block < owned // 2 else [blank, value], axis=0)
 
-    lax.fori_loop(0, owned, hidden_block, 0, unroll=2)
+    lax.fori_loop(0, owned, hidden_block, 0, unroll=4)
     to_right = one_hot(owned * owned, lambda r: (swapped(r & 15) << 4) | (r >> 4))
     pl.semaphore_wait(barrier, 4 + len(partners))
     hidden_copies = exchange(hc, (hs, hs_end), (hr, hr_end), to_right, hid_s, hid_r)
-    lax.fori_loop(0, owned, back_block, 0, unroll=2)
+    lax.fori_loop(0, owned, back_block, 0, unroll=4)
     to_left = one_hot(owned * owned, lambda r: ((r & 15) << 4) | (r >> 4))
     back_copies = exchange(bc, (bs, bs_end), (br, br_end), to_left, back_s, back_r)
 
@@ -227,9 +227,9 @@
 
     left_lane = reduce_lane(1, sl, lo_ref)
     for step in range(half + 2):
+        next(left_lane)
         if step + LEAD < half + 2:
             next(right_lane)
-        next(left_lane)
         if step < half:
             grad_in(step)
     for copy in (*hidden_copies, *back_copies):

time: 87.1 us -> 85.7 us (0.984)
  Pallas kernels: 82.3 us -> 80.8 us
    pallas_call x1, Pallas kernels: 82.3 us -> 80.8 us  [local(): pl.pallas_call(functools.partial(monarch_kernel, scale, rings), out_shape...]
where the time goes in v6:
time: 85.7 us; the launch traced here: 85.3 us
  Pallas kernels  80.8 us (94%)
  local copies, waits for them, and re-layouts  3.88 us (5%)
    pallas_call x1, Pallas kernels, local(): pl.pallas_call(functools.partial(monarch_kernel, scale, rings), out_shape...  80.8 us
    unnamed x1, local copies, waits for them, and re-layouts  2.52 us

profile of v6, /device:TPU:2, one launch (start us, length us, event | category | flops | bytes accessed | tf_op | source)
XLA Modules:
  0.0 85.3 jit_solution(9146121919557286652)
XLA Ops:
  0.6 80.8 %monarch_backward.1 = (bf16[320,2048]{1,0:T(8,128)(2,1)}, f32[32,128]{1,0:T(8,128)}, f32[32,128]{1,0:T(8,128)}) custom-call(bf16[320,2048]{1,0:T(8,128)(2,1)} %x_ref.1, bf16[16,128,128]{2,1,0:T(8,128)(2,1)} %l_ref.1, bf16[16,128,128]{2,1,0:T(8,128)(2,1)} %r_ref.1, bf16[320,2048]{1,0:T(8,128)(2,1)} %g_ref.1), custom_call_target="tpu_custom_call" | custom-call | tf_op jit(solution)/shard_map/monarch_backward/pallas_call | solution.py:252
  81.5 1.4 %copy_bitcast_fusion = (f32[16,2,128]{2,1,0:T(2,128)}, f32[16,2,128]{2,1,0:T(2,128)}) fusion(f32[2,16,128]{2,1,0:T(8,128)} %bitcast.7, f32[2,16,128]{2,1,0:T(8,128)} %bitcast.6), kind=kLoop, calls=%fused_computation | loop fusion | bytes 65536 | tf_op jit(solution)/shard_map/transpose | solution.py:293
  82.8 2.5 %copy.12 = bf16[320,2048]{1,0:T(8,128)(2,1)} copy(bf16[320,2048]{1,0:T(8,128)(2,1)} %get-tuple-element.14) | data formatting | bytes 2621440
